TPU v7x, 512 devices: a whole 4x4x16 slice. The times are simulated.
512 devices in a mesh: lon: 16 (over y, x_lo, core), lat: 32 (over x_hi, z).
Axes of the slice: x: 4 (x_hi: 2, x_lo: 2; x = x_hi * 2 + x_lo), y: 4, z: 16, core: 2. Of those that a mesh axis runs over, the one named last changes fastest.
Arguments:
- tokens: bfloat16 [256, 256, 768], P('lat', 'lon'), may hold values from -6 to 6
- patch_valid: int32 [256, 256], P('lat', 'lon'), may hold values 0 or 1
- block_mask: int32 [32, 16, 16], P('lat', 'lon'), may hold values from 0 to 1, as said below
- gain_attn: float32 [768], replicated, may hold values from 0.1 to 1.9
- gain_mlp: float32 [768], replicated, may hold values from 0.1 to 1.9
- w_qkv: bfloat16 [768, 2304], P('lat'), may hold values from -1.5 to 1.5
- w_out: bfloat16 [768, 768], P('lat'), may hold values from -0.21875 to 0.21875
- w_up: bfloat16 [768, 1536], P('lat'), may hold values from -0.21875 to 0.21875
- w_down: bfloat16 [1536, 768], P('lat'), may hold values from -0.15625 to 0.15625
Outputs:
- mixed: bfloat16 [256, 256, 768], P('lat', 'lon')
Inputs may be any that keep to these rules, and one draw needn't show every extreme that they name: block_mask[s, b, b] is 1 for every strip s and band b.
All inputs are finite; a program needn't handle non-finite values. No bound on the sum of `patch_valid` on one device may be relied on, other than what follows from the above.
Results may differ from a plain program's by a relative error of at most 0.013.
Values may be sent and summed in bfloat16 or wider, within the bound.
No kernel may reach another device: no remote copies, remote signals or barrier semaphores. Data moves between devices by JAX's collectives and lax.ppermute only.
A program may use at most 64 MiB of HBM per device.

v0:
```python
import jax
import jax.numpy as jnp
from jax import lax
from jax.sharding import PartitionSpec as P

D = 768
HEADS = 12
HEAD = 64
HALO = 2
MASKED = -1e30


def with_halo(block, sides, width):
    for axis, dim in sides:
        count = lax.axis_size(axis)
        forward = [(i, i + 1) for i in range(count - 1)]
        backward = [(target, source) for source, target in forward]
        low = lax.ppermute(
            lax.slice_in_dim(block, block.shape[dim] - width, None, axis=dim), axis, forward
        )
        high = lax.ppermute(lax.slice_in_dim(block, 0, width, axis=dim), axis, backward)
        block = jnp.concatenate([low, block, high], axis=dim)
    return block


def layer_norm(inputs, gain_vec):
    centre = jnp.mean(inputs, axis=-1, keepdims=True)
    spread = jnp.mean((inputs - centre) ** 2, axis=-1, keepdims=True)
    return (inputs - centre) * lax.rsqrt(spread + 1e-05) * gain_vec


def attend(running, queries, key_values, allowed):
    maxima, totals, weighted = running
    count_keys = key_values.shape[0]
    key_part = key_values[:, :D].reshape(count_keys, HEADS, HEAD)
    value_part = key_values[:, D:].reshape(count_keys, HEADS, HEAD)
    scores = jnp.einsum("qhd,khd->hqk", queries, key_part, preferred_element_type=jnp.float32)
    scores = jnp.where(allowed[None, None, :], scores, MASKED)
    new_max = jnp.maximum(maxima, jnp.max(scores, axis=-1))
    factor = jnp.exp(maxima - new_max)
    probs = jnp.where(allowed[None, None, :], jnp.exp(scores - new_max[..., None]), 0.0)
    totals = totals * factor + jnp.sum(probs, axis=-1)
    weighted = weighted * factor[..., None] + jnp.einsum(
        "hqk,khd->hqd", probs.astype(jnp.bfloat16), value_part, preferred_element_type=jnp.float32
    )
    return (new_max, totals, weighted)


def body(tokens, patch_valid, block_mask, gain_attn, gain_mlp, w_qkv, w_out, w_up, w_down):
    lat_rows, lon_cols = (tokens.shape[0], tokens.shape[1])
    tile_count = lat_rows * lon_cols
    full_qkv, full_out, full_up, full_down = (
        lax.all_gather(w_qkv, "lat", axis=0, tiled=True),
        lax.all_gather(w_out, "lat", axis=0, tiled=True),
        lax.all_gather(w_up, "lat", axis=0, tiled=True),
        lax.all_gather(w_down, "lat", axis=0, tiled=True),
    )
    residual_in = tokens.reshape(tile_count, D).astype(jnp.float32)
    normed = layer_norm(residual_in, gain_attn).astype(jnp.bfloat16)
    projected = jnp.dot(normed, full_qkv, preferred_element_type=jnp.float32)
    queries = (
        (projected[:, :D] * HEAD ** (-0.5)).astype(jnp.bfloat16).reshape(tile_count, HEADS, HEAD)
    )
    key_values = projected[:, D:].astype(jnp.bfloat16)
    kv_grid = key_values.reshape(lat_rows, lon_cols, 2 * D)
    padded = with_halo(kv_grid, (("lat", 0),), HALO)
    lat_place = lax.axis_index("lat")
    lat_count = lax.axis_size("lat")
    beside = jnp.concatenate([padded[:HALO], padded[lat_rows + HALO :]], axis=0).reshape(
        2 * HALO * lon_cols, 2 * D
    )
    beside_allowed = jnp.concatenate(
        [
            jnp.broadcast_to(lat_place > 0, (HALO * lon_cols,)),
            jnp.broadcast_to(lat_place < lat_count - 1, (HALO * lon_cols,)),
        ],
        axis=0,
    )
    running = (
        jnp.full((HEADS, tile_count), MASKED, jnp.float32),
        jnp.zeros((HEADS, tile_count), jnp.float32),
        jnp.zeros((HEADS, tile_count, HEAD), jnp.float32),
    )
    running = attend(running, queries, beside, beside_allowed)
    mask_row = block_mask.reshape(-1)
    band_total = mask_row.shape[0]
    portion = jax.tree.map(lambda a: lax.all_gather(a, "lon", axis=1, tiled=True), kv_grid)
    count_cols = portion.shape[1]
    channels = portion.shape[2]
    divisor = 1
    for candidate in range(min(count_cols, max(1, 1024 // lat_rows)), 0, -1):
        if count_cols % candidate == 0:
            divisor = candidate
            break
    groups = count_cols // divisor
    bands = (jnp.int32(0) + lax.iota(jnp.int32, count_cols)) // lon_cols
    hits = bands[:, None] == lax.iota(jnp.int32, band_total)[None, :]
    col_ok = (jnp.sum(jnp.where(hits, mask_row[None, :], 0), axis=1) > 0).reshape(groups, divisor)
    blocks = jnp.moveaxis(portion.reshape(lat_rows, groups, divisor, channels), 1, 0)

    def advance(state_now, item):
        block, block_ok = item
        flattened = block.reshape(lat_rows * divisor, channels)
        key_ok = jnp.broadcast_to(block_ok[None, :], (lat_rows, divisor)).reshape(-1)
        return (attend(state_now, queries, flattened, key_ok), None)

    state_out, unused = lax.scan(advance, running, (blocks, col_ok))
    running = state_out
    maxima, totals, weighted = running
    context = weighted / totals[..., None]
    context = jnp.transpose(context, (1, 0, 2)).reshape(tile_count, D).astype(jnp.bfloat16)
    validity = patch_valid.reshape(tile_count, 1).astype(jnp.float32)
    attended = jnp.dot(context, full_out, preferred_element_type=jnp.float32)
    hidden_state = (residual_in + validity * attended).astype(jnp.bfloat16)
    residual = hidden_state.astype(jnp.float32)
    normed_two = layer_norm(residual, gain_mlp).astype(jnp.bfloat16)
    inner = jax.nn.gelu(jnp.dot(normed_two, full_up, preferred_element_type=jnp.float32)).astype(
        jnp.bfloat16
    )
    mixed = residual + validity * jnp.dot(inner, full_down, preferred_element_type=jnp.float32)
    return mixed.astype(jnp.bfloat16).reshape(lat_rows, lon_cols, D)


def solution(mesh):
    in_specs = (
        P("lat", "lon", None),
        P("lat", "lon"),
        P("lat", "lon", None),
        P(),
        P(),
        P("lat", None),
        P("lat", None),
        P("lat", None),
        P("lat", None),
    )
    out_specs = P("lat", "lon", None)
    return jax.shard_map(body, mesh=mesh, in_specs=in_specs, out_specs=out_specs, check_vma=False)
```

profile of v0, /device:TPU:8, one launch (start us, length us, event | category | flops | bytes accessed | tf_op | source)
XLA Modules:
  0.0 680.6 jit_solution(9554029814059372410)
XLA Ops:
  6.5 0.7 all-gather.6.cloned.1.call-update
  7.3 0.0 all-gather.8.cloned.1.call-start
  7.3 1.0 convert_reduce_fusion
  8.3 0.1 div.31
  8.4 1.1 multiply_reduce_fusion.1
  9.6 0.1 rsqrt.20
  9.6 1.1 fusion.30
  10.8 164.0 %all-gather.6.cloned.1.call-done = bf16[768,2304]{1,0:T(8,128)(2,1)} async-done(((bf16[24,2304]{1,0:T(8,128)(2,1)}), bf16[768,2304]{1,0:T(8,128)(2,1)}) %all-gather.6.cloned.1.call-update) | async-done | bytes 3538960 | tf_op jit(solution)/shard_map/all_gather | solution.py:53
  174.7 2.6 fusion.58
  177.4 0.8 slice.48
  178.2 0.0 all-gather.8.cloned.1.call-update
  178.2 0.0 all-gather.10.cloned.1.call-start
  178.3 0.7 all-gather.10.cloned.1.call-update
  178.9 0.0 all-gather.12.cloned.1.call-start
  179.0 0.5 all-gather.12.cloned.1.call-update
  179.5 0.0 all-gather.14.cloned.1.call-start
  179.6 0.5 all-gather.14.cloned.1.call-update
  180.1 0.1 select_reduce_fusion
  180.2 0.6 compare_bitcast_fusion
  180.8 0.7 convert_element_type.61
  181.5 3.7 collective-permute-start
  185.2 1.3 collective-permute-start.1
  186.5 0.2 copy.20
  186.7 0.7 collective-permute-done
  187.4 4.3 collective-permute-done.1
  191.7 0.2 reshape.127
  191.9 0.2 fusion.59
  192.1 0.1 fusion.36
  192.2 0.6 exponential_multiply_fusion
  192.8 0.2 copy.22
  193.0 1.0 convolution_add_fusion
  194.0 29.0 %all-gather.8.cloned.1.call-done = bf16[8,256,1536]{2,1,0:T(8,128)(2,1)} async-done(((bf16[8,16,1536]{2,1,0:T(8,128)(2,1)}), bf16[8,256,1536]{2,1,0:T(8,128)(2,1)}) %all-gather.8.cloned.1.call-update) | async-done | bytes 6291472 | tf_op jit(solution)/shard_map/all_gather | solution.py:87
  223.0 35.1 %while.14 = (s32[]{:T(128)}, f32[12,128]{1,0:T(8,128)S(1)}, f32[12,128]{1,0:T(8,128)}, f32[12,128,64]{1,2,0:T(8,128)}, pred[2,128]{1,0:T(4,128)(4,1)}, /*index=5...) while((s32[]{:T(128)}, f32[12,128]{1,0:T(8,128)S(1)}, f32[12,128]{1,0:T(8,128)}, ...), condition=%wide.region_8.9_spmd, body=%wide.region_5.8_spmd.sunk | while | flops 418581504 | bytes 67224168 | solution.py:107
  223.0 0.7 dynamic-slice_bitcast_fusion.2
  223.7 2.1 constant_dynamic-slice_fusion.2
  225.9 1.4 fusion.83
  227.2 1.7 copy.35
  228.9 1.4 bitcast_reduce_fusion.2
  230.4 0.0 copy-start.2
  230.4 2.5 fusion.84
  233.0 0.1 copy-done
  233.0 0.6 multiply_add_fusion.2
  233.7 0.6 copy-done.3
  234.3 0.7 copy.36
  235.0 5.6 fusion.85
  240.6 0.7 dynamic-slice_bitcast_fusion.2
  241.3 2.1 constant_dynamic-slice_fusion.2
  243.4 1.4 fusion.83
  244.8 1.7 copy.35
  246.5 1.4 bitcast_reduce_fusion.2
  247.9 0.0 copy-start.2
  248.0 2.5 fusion.84
  250.5 0.1 copy-done
  250.6 0.6 multiply_add_fusion.2
  251.2 0.6 copy-done.3
  251.8 0.7 copy.36
  252.6 5.6 fusion.85
  258.1 1.0 divide_convert_fusion
  259.2 112.0 %all-gather.10.cloned.1.call-done = bf16[768,768]{1,0:T(8,128)(2,1)} async-done(((bf16[24,768]{1,0:T(8,128)(2,1)}), bf16[768,768]{1,0:T(8,128)(2,1)}) %all-gather.10.cloned.1.call-update) | async-done | bytes 1179664 | tf_op jit(solution)/shard_map/all_gather | solution.py:54
  371.2 1.7 fusion.60
  373.0 0.2 multiply_reduce_fusion
  373.2 147.3 %all-gather.12.cloned.1.call-done = bf16[768,1536]{1,0:T(8,128)(2,1)} async-done(((bf16[24,1536]{1,0:T(8,128)(2,1)}), bf16[768,1536]{1,0:T(8,128)(2,1)}) %all-gather.12.cloned.1.call-update) | async-done | bytes 2359312 | tf_op jit(solution)/shard_map/all_gather | solution.py:55
  520.4 149.6 %all-gather.14.cloned.1.call-done = bf16[1536,768]{1,0:T(8,128)(2,1)} async-done(((bf16[48,768]{1,0:T(8,128)(2,1)}), bf16[1536,768]{1,0:T(8,128)(2,1)}) %all-gather.14.cloned.1.call-update) | async-done | bytes 2359312 | tf_op jit(solution)/shard_map/all_gather | solution.py:56
  670.0 4.1 fusion.17
  (44 shorter events, 0.2 us)
Async XLA Ops:
  6.5 168.2 %all-gather.6.cloned.1.call-start = ((), (), s32[]{:S(2)}) async-start(), calls=%async_computation | async-start | bytes 3649536 | tf_op jit(solution)/shard_map/all_gather | solution.py:53
  7.3 215.8 %all-gather.8.cloned.1.call-start = ((), (), s32[]{:S(2)}) async-start(), calls=%async_computation.1 | async-start | bytes 6684672 | tf_op jit(solution)/shard_map/all_gather | solution.py:87
  10.7 169.4 %copy-start.8 = (s32[1,1,16]{2,1,0:T(1,128)S(1)}, s32[1,1,16]{2,1,0:T(1,128)}, u32[]{:S(2)}) copy-start(s32[1,1,16]{2,1,0:T(1,128)} %param.13) | copy-start | bytes 196
  10.8 170.0 %copy-start.6 = (s32[8,16]{1,0:T(8,128)S(1)}, s32[8,16]{1,0:T(8,128)}, u32[]{:S(2)}) copy-start(s32[8,16]{1,0:T(8,128)} %param.12) | copy-start | bytes 1540
  178.2 193.0 %all-gather.10.cloned.1.call-start = ((), (), s32[]{:S(2)}) async-start(), calls=%async_computation.2 | async-start | bytes 1216512 | tf_op jit(solution)/shard_map/all_gather | solution.py:54
  178.9 341.5 %all-gather.12.cloned.1.call-start = ((), (), s32[]{:S(2)}) async-start(), calls=%async_computation.3 | async-start | bytes 2433024 | tf_op jit(solution)/shard_map/all_gather | solution.py:55
  179.5 490.5 %all-gather.14.cloned.1.call-start = ((), (), s32[]{:S(2)}) async-start(), calls=%async_computation.4 | async-start | bytes 2433024 | tf_op jit(solution)/shard_map/all_gather | solution.py:56
  181.5 5.9 collective-permute-start
  185.2 6.5 collective-permute-start.1
  223.0 148.2 %copy-start.1 = (bf16[8,16,768]{2,1,0:T(8,128)(2,1)S(1)}, bf16[8,16,768]{2,1,0:T(8,128)(2,1)}, u32[]{:S(2)}) copy-start(bf16[8,16,768]{2,1,0:T(8,128)(2,1)} %param.11) | copy-start | bytes 589828
  223.7 5.2 copy-start.4
  230.4 2.7 copy-start
  230.4 2.6 copy-start.2
  233.7 0.6 copy-start.3
  233.7 1.4 copy-start.5
  241.3 5.2 copy-start.4
  247.9 2.7 copy-start
  247.9 2.6 copy-start.2
  251.2 0.6 copy-start.3
  251.2 1.4 copy-start.5
  258.1 411.9 %copy-start.7 = (f32[128]{0:T(128)S(1)}, f32[128]{0:T(128)}, u32[]{:S(2)}) copy-start(f32[128]{0:T(128)} %convert_element_type.61) | copy-start | bytes 1540
  258.1 411.9 %copy-start.9 = (f32[768]{0:T(1024)S(1)}, f32[768]{0:T(1024)}, u32[]{:S(2)}) copy-start(f32[768]{0:T(1024)} %param.15) | copy-start | bytes 9220
Sparse Core Ops, SparseCore 0:
  10.5 164.2 all-gather.5
  178.3 44.6 all-gather.7
  226.1 145.0 all-gather.9
  374.2 146.2 all-gather.11
  523.4 146.6 all-gather.13
where the time goes:
time: 681 us
  waiting for transfers between devices  609 us (89%)
  matrix products  23.7 us (3%)
  local copies, waits for them, and re-layouts  16.8 us (2%)
  between operations  13.3 us (2%)
  other arithmetic  12.3 us (2%)
    all_gather x1, waiting for transfers between devices, body(): lax.all_gather(w_qkv, 'lat', axis=0, tiled=True)  164 us
    all_gather x1, waiting for transfers between devices, body(): lax.all_gather(w_down, 'lat', axis=0, tiled=True)  150 us
    all_gather x1, waiting for transfers between devices, body(): lax.all_gather(w_up, 'lat', axis=0, tiled=True)  147 us
    all_gather x1, waiting for transfers between devices, body(): lax.all_gather(w_out, 'lat', axis=0, tiled=True)  112 us
    all_gather x1, waiting for transfers between devices, body(): lax.all_gather(a, 'lon', axis=1, tiled=True)  29 us
  transfers between devices with their start and end apart: 7, of which 7 were waited for; matrix products, arithmetic and copies ran while one was open for 6% of the time, Pallas kernels for 0%

commit v1 on v0

--- a/solution.py
+++ b/solution.py
@@ -52,7 +52,9 @@
     full_qkv, full_out, full_up, full_down = (
         lax.all_gather(w_qkv, "lat", axis=0, tiled=True),
         lax.all_gather(w_out, "lat", axis=0, tiled=True),
-        lax.all_gather(w_up, "lat", axis=0, tiled=True),
+        jnp.concatenate(
+            lax.all_to_all(jnp.stack([w_up] * lax.axis_size("lat")), "lat", 0, 0), axis=0
+        ),
         lax.all_gather(w_down, "lat", axis=0, tiled=True),
     )
     residual_in = tokens.reshape(tile_count, D).astype(jnp.float32)

time: 681 us -> 549 us (0.81)
  waiting for transfers between devices: 609 us -> 469 us
  starting transfers between devices: 5.11 us -> 13.1 us
    all_gather x1 -> x0, waiting for transfers between devices: 147 us -> none  [body(): lax.all_gather(w_up, 'lat', axis=0, tiled=True)]
    ppermute x1, waiting for transfers between devices: 0.69 us -> 85.9 us  [with_halo(): lax.ppermute(lax.slice_in_dim(block, block.shape[dim] - width, None, axis...]
    all_gather x1, waiting for transfers between devices: 112 us -> 66.9 us  [body(): lax.all_gather(w_out, 'lat', axis=0, tiled=True)]
    all_gather x1, waiting for transfers between devices: 29 us -> 0.01 us  [body(): lax.all_gather(a, 'lon', axis=1, tiled=True)]
    all_to_all x0 -> x1, starting transfers between devices: none -> 8.05 us  [body(): lax.all_to_all(jnp.stack([w_up] * lax.axis_size('lat')), 'lat', 0, 0)]
  transfers between devices with their start and end apart: 7 -> 7, of which waited for: 7 -> 5; matrix products, arithmetic and copies ran while one was open for 6% -> 8% of each run, Pallas kernels for 0% -> 0%
where the time goes in v1:
time: 549 us
  waiting for transfers between devices  469 us (85%)
  matrix products  23.1 us (4%)
  local copies, waits for them, and re-layouts  18.4 us (3%)
  between operations  13.3 us (2%)
  starting transfers between devices  13.1 us (2%)
  other arithmetic  12 us (2%)
    all_gather x1, waiting for transfers between devices, body(): lax.all_gather(w_qkv, 'lat', axis=0, tiled=True)  164 us
    all_gather x1, waiting for transfers between devices, body(): lax.all_gather(w_down, 'lat', axis=0, tiled=True)  147 us
    ppermute x1, waiting for transfers between devices, with_halo(): lax.ppermute(lax.slice_in_dim(block, block.shape[dim] - width, None, axis...  85.9 us
    all_gather x1, waiting for transfers between devices, body(): lax.all_gather(w_out, 'lat', axis=0, tiled=True)  66.9 us
    dot_general x3, matrix products, attend(): jnp.einsum('hqk,khd->hqd', probs.astype(jnp.bfloat16), value_part, prefer...  11.6 us
  transfers between devices with their start and end apart: 7, of which 5 were waited for; matrix products, arithmetic and copies ran while one was open for 8% of the time, Pallas kernels for 0%

profile of v1, /device:TPU:8, one launch (start us, length us, event | category | flops | bytes accessed | tf_op | source)
XLA Modules:
  0.0 548.8 jit_solution(6821103623028189184)
XLA Ops:
  6.5 0.7 all-gather.5.cloned.1.call-update
  7.3 0.0 all-gather.7.cloned.1.call-start
  7.3 1.0 convert_reduce_fusion
  8.3 0.1 div.31
  8.4 1.1 multiply_reduce_fusion.1
  9.6 0.1 rsqrt.20
  9.6 1.1 fusion.30
  10.7 0.0 copy-start.6
  10.8 164.0 %all-gather.5.cloned.1.call-done = bf16[768,2304]{1,0:T(8,128)(2,1)} async-done(((bf16[24,2304]{1,0:T(8,128)(2,1)}), bf16[768,2304]{1,0:T(8,128)(2,1)}) %all-gather.5.cloned.1.call-update) | async-done | bytes 3538960 | tf_op jit(solution)/shard_map/all_gather | solution.py:53
  174.7 2.6 fusion.58
  177.4 0.8 slice.48
  178.2 0.0 all-gather.7.cloned.1.call-update
  178.2 0.0 all-gather.9.cloned.1.call-start
  178.3 0.7 all-gather.9.cloned.1.call-update
  179.0 1.6 stack.2
  180.5 8.0 %all-to-all-start = ((bf16[32,24,1536]{2,1,0:T(8,128)(2,1)}), bf16[32,24,1536]{2,1,0:T(8,128)(2,1)}, u32[]{:S(2)}, u32[]{:S(2)}) async-start(bf16[32,24,1536]{2,1,0:T(8,128)(2,1)} %stack.2), calls=%async_computation | async-start | bytes 4718592 | tf_op jit(solution)/shard_map/all_to_all | solution.py:56
  188.6 0.0 all-gather.11.cloned.1.call-start
  188.6 0.5 all-gather.11.cloned.1.call-update
  189.2 0.7 convert_element_type.61
  189.9 0.1 select_reduce_fusion
  190.0 0.5 compare_bitcast_fusion
  190.5 3.6 collective-permute-start
  194.1 1.3 collective-permute-start.1
  195.5 0.2 copy.20
  195.6 85.9 %collective-permute-done = bf16[2,16,1536]{2,1,0:T(8,128)(2,1)S(1)} collective-permute-done((bf16[2,16,1536]{2,1,0:T(8,128)(2,1)S(1)}, bf16[2,16,1536]{2,1,0:T(8,128)(2,1)S(1)}, u32[]{:S(2)}, u32[]{:S(2)}) %collective-permute-start) | collective-permute-done | bytes 98336 | tf_op jit(solution)/shard_map/ppermute | solution.py:18
  281.5 2.7 collective-permute-done.1
  284.3 0.2 reshape.132
  284.5 0.2 copy.22
  284.7 0.2 fusion.59
  284.9 0.1 fusion.36
  285.0 0.6 exponential_multiply_fusion
  285.6 1.0 convolution_add_fusion
  286.6 34.4 %while.14 = (s32[]{:T(128)}, f32[12,128]{1,0:T(8,128)S(1)}, f32[12,128]{1,0:T(8,128)}, f32[12,128,64]{1,2,0:T(8,128)}, pred[2,128]{1,0:T(4,128)(4,1)}, /*index=5...) while((s32[]{:T(128)}, f32[12,128]{1,0:T(8,128)S(1)}, f32[12,128]{1,0:T(8,128)}, ...), condition=%wide.region_8.9_spmd, body=%wide.region_5.8_spmd.sunk | while | flops 418581504 | bytes 67224168 | solution.py:109
  286.6 0.6 dynamic-slice_bitcast_fusion.2
  287.3 2.1 constant_dynamic-slice_fusion.2
  289.4 1.4 fusion.83
  290.7 1.7 copy.35
  292.5 1.4 bitcast_reduce_fusion.2
  293.9 0.0 copy-start.2
  294.0 2.5 fusion.84
  296.4 0.1 copy-done
  296.6 0.6 multiply_add_fusion.2
  297.2 0.6 copy-done.3
  297.8 0.7 copy.36
  298.5 5.3 fusion.85
  303.8 0.6 dynamic-slice_bitcast_fusion.2
  304.5 2.1 constant_dynamic-slice_fusion.2
  306.6 1.4 fusion.83
  307.9 1.7 copy.35
  309.7 1.4 bitcast_reduce_fusion.2
  311.1 0.0 copy-start.2
  311.1 2.5 fusion.84
  313.6 0.1 copy-done
  313.8 0.6 multiply_add_fusion.2
  314.4 0.6 copy-done.3
  315.0 0.7 copy.36
  315.7 5.3 fusion.85
  321.0 1.0 divide_convert_fusion
  322.1 66.9 %all-gather.9.cloned.1.call-done = bf16[768,768]{1,0:T(8,128)(2,1)} async-done(((bf16[24,768]{1,0:T(8,128)(2,1)}), bf16[768,768]{1,0:T(8,128)(2,1)}) %all-gather.9.cloned.1.call-update) | async-done | bytes 1179664 | tf_op jit(solution)/shard_map/all_gather | solution.py:54
  389.0 1.7 fusion.60
  390.7 0.2 multiply_reduce_fusion
  390.9 147.3 %all-gather.11.cloned.1.call-done = bf16[1536,768]{1,0:T(8,128)(2,1)} async-done(((bf16[48,768]{1,0:T(8,128)(2,1)}), bf16[1536,768]{1,0:T(8,128)(2,1)}) %all-gather.11.cloned.1.call-update) | async-done | bytes 2359312 | tf_op jit(solution)/shard_map/all_gather | solution.py:58
  538.2 0.0 all-to-all-done
  538.2 4.1 fusion.17
  (46 shorter events, 0.2 us)
Async XLA Ops:
  6.5 168.2 %all-gather.5.cloned.1.call-start = ((), (), s32[]{:S(2)}) async-start(), calls=%async_computation.1 | async-start | bytes 3649536 | tf_op jit(solution)/shard_map/all_gather | solution.py:53
  7.3 279.4 %all-gather.7.cloned.1.call-start = ((), (), s32[]{:S(2)}) async-start(), calls=%async_computation.2 | async-start | bytes 6684672 | tf_op jit(solution)/shard_map/all_gather | solution.py:89
  10.7 168.2 %copy-start.6 = (bf16[24,1536]{1,0:T(8,128)(2,1)S(1)}, bf16[24,1536]{1,0:T(8,128)(2,1)}, u32[]{:S(2)}) copy-start(bf16[24,1536]{1,0:T(8,128)(2,1)} %param.18) | copy-start | bytes 221188
  178.2 210.8 %all-gather.9.cloned.1.call-start = ((), (), s32[]{:S(2)}) async-start(), calls=%async_computation.3 | async-start | bytes 1216512 | tf_op jit(solution)/shard_map/all_gather | solution.py:54
  180.5 8.7 %copy-start.7 = (s32[8,16]{1,0:T(8,128)S(1)}, s32[8,16]{1,0:T(8,128)}, u32[]{:S(2)}) copy-start(s32[8,16]{1,0:T(8,128)} %param.12) | copy-start | bytes 1540
  180.5 9.3 %copy-start.9 = (s32[1,1,16]{2,1,0:T(1,128)S(1)}, s32[1,1,16]{2,1,0:T(1,128)}, u32[]{:S(2)}) copy-start(s32[1,1,16]{2,1,0:T(1,128)} %param.13) | copy-start | bytes 196
  180.5 357.7 %all-to-all-start = ((bf16[32,24,1536]{2,1,0:T(8,128)(2,1)}), bf16[32,24,1536]{2,1,0:T(8,128)(2,1)}, u32[]{:S(2)}, u32[]{:S(2)}) async-start(bf16[32,24,1536]{2,1,0:T(8,128)(2,1)} %stack.2), calls=%async_computation | async-start | bytes 4718592 | tf_op jit(solution)/shard_map/all_to_all | solution.py:56
  188.6 349.6 %all-gather.11.cloned.1.call-start = ((), (), s32[]{:S(2)}) async-start(), calls=%async_computation.4 | async-start | bytes 2433024 | tf_op jit(solution)/shard_map/all_gather | solution.py:58
  190.5 91.1 %collective-permute-start = (bf16[2,16,1536]{2,1,0:T(8,128)(2,1)S(1)}, bf16[2,16,1536]{2,1,0:T(8,128)(2,1)S(1)}, u32[]{:S(2)}, u32[]{:S(2)}) collective-permute-start(bf16[2,16,1536]{2,1,0:T(8,128)(2,1)S(1)} %bitcast.92), channel_id=1, source_target_pairs={{0,1},{1,2},{2,3},{3,4},{4,5},{5,6},{6,7},{7,8},{8,9},{9,10},{10,1... | collective-permute-start | bytes 294920 | tf_op jit(solution)/shard_map/ppermute | solution.py:18
  194.1 90.1 %collective-permute-start.1 = (bf16[2,16,1536]{2,1,0:T(8,128)(2,1)S(1)}, bf16[2,16,1536]{2,1,0:T(8,128)(2,1)S(1)}, u32[]{:S(2)}, u32[]{:S(2)}) collective-permute-start(bf16[2,16,1536]{2,1,0:T(8,128)(2,1)S(1)} %bitcast.91), channel_id=1, source_target_pairs={{1,0},{2,1},{3,2},{4,3},{5,4},{6,5},{7,6},{8,7},{9,8},{10,9},{11,1... | collective-permute-start | bytes 294920 | tf_op jit(solution)/shard_map/ppermute | solution.py:21
  286.6 102.4 %copy-start.1 = (bf16[8,16,768]{2,1,0:T(8,128)(2,1)S(1)}, bf16[8,16,768]{2,1,0:T(8,128)(2,1)}, u32[]{:S(2)}) copy-start(bf16[8,16,768]{2,1,0:T(8,128)(2,1)} %param.11) | copy-start | bytes 589828
  287.3 5.2 copy-start.4
  293.9 2.7 copy-start
  293.9 2.6 copy-start.2
  297.2 0.6 copy-start.3
  297.2 1.4 copy-start.5
  304.4 5.2 copy-start.4
  311.1 2.7 copy-start
  311.1 2.6 copy-start.2
  314.4 0.6 copy-start.3
  314.4 1.4 copy-start.5
  321.0 217.2 %copy-start.8 = (f32[128]{0:T(128)S(1)}, f32[128]{0:T(128)}, u32[]{:S(2)}) copy-start(f32[128]{0:T(128)} %convert_element_type.61) | copy-start | bytes 1540
  321.0 217.2 %copy-start.10 = (f32[768]{0:T(1024)S(1)}, f32[768]{0:T(1024)}, u32[]{:S(2)}) copy-start(f32[768]{0:T(1024)} %param.15) | copy-start | bytes 9220
Sparse Core Ops, SparseCore 0:
  10.5 164.2 all-gather.4
  178.3 51.2 all-gather.6
  232.8 156.1 all-gather.8
  391.9 146.2 all-gather.10
